TPU v7x, 128 devices: a whole 4x4x4 slice. The times are simulated.
128 devices in a mesh: row: 8 (over y, core), col: 16 (over x, z).
Axes of the slice: x: 4, y: 4, z: 4, core: 2. Of those that a mesh axis runs over, the one named last changes fastest.
Arguments:
- valence_bands: bfloat16 [256, 96, 9216], P(('row', 'col')), may hold values from -6 to 6
- conduction_bands: bfloat16 [256, 96, 9216], P(('row', 'col')), may hold values from -6 to 6
- valence_energy: float32 [256], P(('row', 'col')), may hold values from -8 to -0.5
- conduction_energy: float32 [256], P(('row', 'col')), may hold values from 0.5 to 8
- pair_valence: int32 [128, 4], P(('row', 'col')), may hold values from 0 to 1
- pair_conduction: int32 [128, 4], P(('row', 'col')), may hold values from 0 to 1
- pair_count: int32 [128], replicated, may hold values from 1 to 4, 256 in all
- stick_perm: int32 [160], replicated, may hold values from 0 to 159, each once
Outputs:
- response: float32 [20480, 20480], P('row', 'col')
Inputs may be any that keep to these rules, and one draw needn't show every extreme that they name: `pair_count`: the numbers sum to 256 and the largest is 4. `stick_perm`: A permutation of the box sticks.
All inputs are finite; a program needn't handle non-finite values.
Results may differ from a plain program's by a relative error of at most 0.0003.
Values sent between devices are 32-bit elements; how exact they have to be, the bound alone decides.
No kernel may reach another device: no remote copies, remote signals or barrier semaphores. Data moves between devices by JAX's collectives and lax.ppermute only.
A program may use at most 128 MiB of HBM per device.

v0:
```python
import functools
import math

import jax
import jax.numpy as jnp
import numpy as np
from jax import lax
from jax.experimental import pallas as pl
from jax.experimental.pallas import tpu as pltpu
from jax.sharding import Mesh, PartitionSpec as P

NG = 96
KX = 10
KY = 16
KZ = 64
CAP = 4
NSTICK = 160
LANES = 128
NY, NCORE, NX, NZ = 4, 2, 4, 4
DEVICES = 128
PAIRS = 256
AXIS = {"y": NY, "core": NCORE, "x": NX, "z": NZ}

YL = 4
NB = NG // YL
Q = YL * NG
TERMS = 2
GROWS = 24
BCHUNK = 8
STEPS = NB // BCHUNK
CHUNK = BCHUNK * Q
F32 = jnp.float32
BF16 = jnp.bfloat16


def split_np(table):
    table = np.asarray(table, np.float32)
    high = table.astype(jnp.bfloat16)
    low = (table - high.astype(np.float32)).astype(jnp.bfloat16)
    return high, low


def tables():
    x = np.arange(NG)
    gx = np.arange(1, KX + 1)
    angle = 2 * math.pi / NG * ((gx[:, None] * x[None, :]) % NG)
    factor = np.zeros((GROWS, NG))
    for i in range(KX):
        factor[8 * (i // 4) + i % 4] = np.cos(angle[i])
        factor[8 * (i // 4) + 4 + i % 4] = -np.sin(angle[i])
    high, low = split_np(factor)
    x_table = np.concatenate([np.tile(high, (1, TERMS)), np.tile(low, (1, TERMS))], 0)
    b = np.arange(NB)
    gy = np.arange(KY)
    phi = 2 * math.pi / NB * ((gy[:, None] * b[None, :]) % NB)
    mix = np.zeros((2, 4, KY, NB, 8))
    for i in range(4):
        mix[0, i, :, :, i] = np.cos(phi)
        mix[0, i, :, :, 4 + i] = np.sin(phi)
        mix[1, i, :, :, 4 + i] = np.cos(phi)
        mix[1, i, :, :, i] = -np.sin(phi)
    mix = np.concatenate(split_np(mix.reshape(128, NB * 8)), 0)
    q = np.arange(Q)
    twist = 2 * math.pi / NG * (gy[:, None] * (q // NG)[None, :])
    twist = np.stack([np.cos(twist), np.sin(twist)]).astype(np.float32)
    gz = np.arange(KZ)
    theta = 2 * math.pi / NG * (((q % NG)[:, None] * gz[None, :]) % NG)
    cosine, sine = np.cos(theta), np.sin(theta)
    z_table = np.concatenate(
        [np.concatenate([cosine, -sine], 1), np.concatenate([sine, cosine], 1)], 0
    )
    z_table = np.concatenate(split_np(z_table), 1)
    return x_table, mix, twist, z_table


def split(value):
    high = value.astype(BF16)
    low = (value - high.astype(F32)).astype(BF16)
    return high, low


def dot(left, right):
    return jnp.dot(left, right, preferred_element_type=F32)


def lane_group(rows):
    return lax.broadcasted_iota(jnp.int32, (rows, LANES), 1) // 32


def quarters(sticks_2d, q, start, count, stride):
    total = None
    for k in range(CAP):
        part = sticks_2d[pl.ds(8 * start + k, count, stride=8 * stride), :]
        turn = (32 * (k - q)) % LANES
        moved = pltpu.roll(part, turn, 1) if turn else part
        total = moved if total is None else jnp.where(lane_group(count) == k, moved, total)
    return total


def pack(sticks_2d, out):
    for q in range(4):
        for s in range(5):
            value = quarters(sticks_2d, q, s, 32, 5)
            for y in range(4):
                start = 10 * (32 * y + q) + s
                out[pl.ds(start, 4, stride=40), :] = value[8 * y : 8 * y + 4]
                start = 10 * (32 * y + 16 + 4 * q) + s
                out[pl.ds(start, 4, stride=10), :] = value[8 * y + 4 : 8 * y + 8]
            for h in range(2):
                out[pl.ds(10 * (32 * q + 16 * h) + 5 + s, 16, stride=10), :] = quarters(
                    sticks_2d, q, 5 * h + s, 16, 10
                )


def transform_kernel(
    slot_v,
    slot_c,
    perm,
    energy_v,
    energy_c,
    v_ref,
    c_ref,
    x_table,
    mix,
    twist,
    z_table,
    out,
    zh,
    zl,
    natural,
    ordered,
    v_wide,
    c_wide,
):
    step = pl.program_id(0)
    v_wide[...] = v_ref[...].astype(F32)
    c_wide[...] = c_ref[...].astype(F32)
    for k in range(CAP):
        high, low = split(v_wide[slot_v[0, k]] * c_wide[slot_c[0, k]])
        x_part = dot(x_table[...], jnp.concatenate([high, low], 0))
        x_part = x_part[:GROWS] + x_part[GROWS:]
        for g in range(3):
            block = x_part[8 * g : 8 * g + 8]
            block = jnp.concatenate(
                [block[:, Q * i : Q * i + Q] for i in range(BCHUNK)], 0
            )
            row = pl.multiple_of(step * (8 * BCHUNK), 16)
            high, low = split(block)
            zh[g, pl.ds(row, 8 * BCHUNK), Q * k : Q * (k + 1)] = high
            zl[g, pl.ds(row, 8 * BCHUNK), Q * k : Q * (k + 1)] = low

    @pl.when(step == STEPS - 1)
    def _():
        turn_c = twist[0][None]
        turn_s = twist[1][None]
        for k in range(CAP):
            real, imag = [], []
            for g in range(3):
                mixed = dot(mix[...], zh[g, :, Q * k : Q * (k + 1)])
                mixed = mixed[:128] + mixed[128:]
                mixed += dot(mix[:128], zl[g, :, Q * k : Q * (k + 1)])
                count = 64 if g < 2 else 32
                real.append(mixed[:count])
                imag.append(mixed[64 : 64 + count])
            real = jnp.concatenate(real, 0).reshape(KX, KY, Q)
            imag = jnp.concatenate(imag, 0).reshape(KX, KY, Q)
            turned_real = (real * turn_c + imag * turn_s).reshape(NSTICK, Q)
            turned_imag = (imag * turn_c - real * turn_s).reshape(NSTICK, Q)
            high, low = split(jnp.concatenate([turned_real, turned_imag], 1))
            value = dot(high, z_table[...])
            value = value[:, :128] + value[:, 128:] + dot(low, z_table[:, :128])
            gap = energy_c[slot_c[0, k]] - energy_v[slot_v[0, k]]
            gap = jnp.full((1, LANES), gap, F32)
            value = value * (jnp.sqrt(1.0 / gap) * NG ** (-1.5))
            natural[pl.ds(k, NSTICK, stride=8), :] = value

        def move(s, carry):
            source = pl.multiple_of(8 * perm[s], 8)
            target = pl.multiple_of(8 * s, 8)
            ordered[pl.ds(target, 8), :] = natural[pl.ds(source, 8), :]
            return carry

        lax.fori_loop(0, NSTICK, move, 0, unroll=8)
        pack(ordered, out)


def transform(v, c, ev, ec, slot_v, slot_c, perm):
    consts = [jnp.asarray(t) for t in tables()]
    whole = lambda a: pl.BlockSpec(a.shape, lambda i, *_: (0,) * a.ndim)
    bands = pl.BlockSpec((2, NG, CHUNK), lambda i, *_: (0, 0, i))
    return pl.pallas_call(
        transform_kernel,
        name="transform",
        out_shape=jax.ShapeDtypeStruct((10 * DEVICES, LANES), F32),
        grid_spec=pltpu.PrefetchScalarGridSpec(
            num_scalar_prefetch=5,
            grid=(STEPS,),
            in_specs=[bands, bands] + [whole(t) for t in consts],
            out_specs=pl.BlockSpec((10 * DEVICES, LANES), lambda i, *_: (0, 0)),
            scratch_shapes=[
                pltpu.VMEM((3, NB * 8, CAP * Q), BF16),
                pltpu.VMEM((3, NB * 8, CAP * Q), BF16),
                pltpu.VMEM((8 * NSTICK, LANES), F32),
                pltpu.VMEM((8 * NSTICK, LANES), F32),
                pltpu.VMEM((2, NG, CHUNK), F32),
                pltpu.VMEM((2, NG, CHUNK), F32),
            ],
        ),
        cost_estimate=pl.CostEstimate(
            flops=4_000_000_000,
            bytes_accessed=9_000_000,
            transcendentals=0,
        ),
    )(slot_v, slot_c, perm, ev, ec, v, c, *consts)


def pieces_kernel(count_ref, x_ref, row_out, col_out):
    counts = jnp.broadcast_to(count_ref[...], (DEVICES, LANES))
    device = lax.broadcasted_iota(jnp.int32, (DEVICES, LANES), 0)
    lane = lax.broadcasted_iota(jnp.int32, (DEVICES, LANES), 1)
    offset = jnp.sum(jnp.where(lane < device, counts, 0), axis=1, keepdims=True)
    own = jnp.sum(jnp.where(lane == device, counts, 0), axis=1, keepdims=True)
    pair = lax.broadcasted_iota(jnp.int32, (DEVICES, PAIRS), 1)
    chosen = []
    for k in range(CAP):
        hit = jnp.logical_and(pair == offset + k, k < own)
        chosen.append(jnp.where(hit, 1.0, 0.0).astype(BF16))
    chosen = jnp.concatenate(chosen + chosen, 0)
    wide = []
    for s in range(10):
        turned = x_ref[pl.ds(s, DEVICES, stride=10), :].T
        wide.append(
            jnp.concatenate([turned[32 * k : 32 * k + 32] for k in range(CAP)], 1)
        )
    high, low = split(jnp.concatenate(wide, 0))
    total = dot(jnp.concatenate([high, low], 1), chosen)
    row_out[...] = total[:160]
    col_out[...] = total[160:]


def pieces(count, received):
    shape = jax.ShapeDtypeStruct((160, PAIRS), F32)
    return pl.pallas_call(
        pieces_kernel,
        name="pieces",
        compiler_params=pltpu.CompilerParams(vmem_limit_bytes=12 << 20),
        out_shape=(shape, shape),
        cost_estimate=pl.CostEstimate(
            flops=180_000_000, bytes_accessed=1_000_000, transcendentals=0
        ),
    )(count, received)


def columns_kernel(where, mine, theirs, out, flat):
    y, core = where[1], where[2]
    for other, source in enumerate((mine, theirs)):
        base = 640 * ((core + other) % 2)
        for m in range(4):
            there = (y + 4 - m) % 4
            for s in range(5):
                row = pl.multiple_of(base + 128 * s + 32 * there, 32)
                flat[pl.ds(row, 32), :] = source[m, 32 * s : 32 * s + 32, :]
    for i in range(10):
        high, low = split(-flat[128 * i : 128 * i + 128, :].T)
        out[0:256, 128 * i : 128 * i + 128] = high
        out[256:512, 128 * i : 128 * i + 128] = low
        out[512:768, 128 * i : 128 * i + 128] = high


def columns(where, mine, theirs):
    vmem = pl.BlockSpec(memory_space=pltpu.VMEM)
    return pl.pallas_call(
        columns_kernel,
        name="columns",
        compiler_params=pltpu.CompilerParams(vmem_limit_bytes=16 << 20),
        out_shape=jax.ShapeDtypeStruct((3 * PAIRS, 1280), BF16),
        in_specs=[pl.BlockSpec(memory_space=pltpu.SMEM), vmem, vmem],
        out_specs=vmem,
        scratch_shapes=[pltpu.VMEM((1280, PAIRS), F32)],
        cost_estimate=pl.CostEstimate(
            flops=2_000_000, bytes_accessed=3_000_000, transcendentals=0
        ),
    )(where, mine, theirs)


def product_kernel(count, where, *refs):
    gathered = refs[:count]
    b3, out, a3 = refs[count], refs[-2], refs[-1]
    step = pl.program_id(0)
    part = pl.program_id(1)
    for k in range(count):

        @pl.when(jnp.logical_and(step == k, part == 0))
        def _():
            for m in range(4):
                there = (where[3] + 4 - m) % 4
                for s in range(5):
                    row = pl.multiple_of(128 * s + 32 * there, 32)
                    high, low = split(gathered[k][m, 32 * s : 32 * s + 32, :])
                    a3[pl.ds(row, 32), 0:256] = high
                    a3[pl.ds(row, 32), 256:512] = high
                    a3[pl.ds(row, 32), 512:768] = low

    width = out.shape[1]
    lane = pl.multiple_of(width * part, width)
    for n in range(0, width, 256):
        out[:, n : n + 256] = dot(a3[...], b3[:, pl.ds(lane + n, 256)])


def response_blocks(where, order, gathered, b3, parts, held=None):
    vmem = pl.BlockSpec(memory_space=pltpu.VMEM)
    count = len(gathered)
    width = 1280 // parts

    def place(i, j, w):
        back = sum(jnp.where(i == n, order[n], 0) for n in range(count))
        return ((w[0] + 4 - back) % 4, j)

    extra = [] if held is None else [held]
    return pl.pallas_call(
        functools.partial(product_kernel, count),
        name="response",
        compiler_params=pltpu.CompilerParams(vmem_limit_bytes=24 << 20),
        out_shape=jax.ShapeDtypeStruct((2560, 1280), F32),
        grid_spec=pltpu.PrefetchScalarGridSpec(
            num_scalar_prefetch=1,
            grid=(count, parts),
            in_specs=[vmem] * (count + 1)
            + [pl.BlockSpec(memory_space=pl.ANY)] * len(extra),
            out_specs=pl.BlockSpec((640, width), place),
            scratch_shapes=[pltpu.VMEM((640, 768), BF16)],
        ),
        input_output_aliases={} if held is None else {count + 2: 0},
        cost_estimate=pl.CostEstimate(
            flops=count * 1_300_000_000,
            bytes_accessed=count * 4_000_000,
            transcendentals=0,
        ),
    )(where, *gathered, b3, *extra)


def shift(value, axis, k):
    n = AXIS[axis]
    return lax.ppermute(value, axis, [(i, (i + k) % n) for i in range(n)])


def gather(value, axis):
    got = [value]
    for k in range(1, AXIS[axis]):
        got.append(shift(value, axis, k))
    return got


def plane_gather(value, stage):
    got = [value]
    for k in range(1, 4):
        pairs = []
        for core in range(NCORE):
            for x in range(NX):
                for z in range(NZ):
                    if core == stage:
                        to = (x, (z + k) % NZ)
                    else:
                        to = ((x + k) % NX, z)
                    pairs.append(
                        (16 * core + 4 * x + z, 16 * core + 4 * to[0] + to[1])
                    )
        got.append(lax.ppermute(value, ("core", "x", "z"), pairs))
    return got


def exchange(value):
    value = value.reshape(DEVICES, 10, 1, LANES)
    value = lax.all_to_all(
        value, ("y", "core", "x", "z"), split_axis=0, concat_axis=0, tiled=True
    )
    return value.reshape(DEVICES * 10, LANES)


def compute(v, c, ev, ec, slot_v, slot_c, count, perm):
    packed = transform(v, c, ev, ec, slot_v, slot_c, perm)
    row, column = pieces(count.reshape(1, DEVICES), exchange(packed))
    x, y, core, z = (lax.axis_index(a) for a in ("x", "y", "core", "z"))
    where = jnp.stack([jnp.where(core == 0, x, z), y, core, jnp.where(core == 0, z, x)])
    where = where.astype(jnp.int32)
    row = jnp.stack(plane_gather(row, 0))
    row, column = lax.optimization_barrier((row, column))
    gathered = plane_gather(row, 1)
    mine = jnp.stack(gather(column, "y"))
    b3 = columns(where, mine, shift(mine, "core", 1))
    return response_blocks(where, (0, 1, 3, 2), [gathered[k] for k in (0, 1, 3, 2)], b3, 1)


def solution(mesh):
    fine = Mesh(mesh.devices.reshape(NY, NCORE, NX, NZ), ("y", "core", "x", "z"))
    every = ("y", "core", "x", "z")
    return jax.shard_map(
        compute,
        mesh=fine,
        in_specs=(
            P(every, None, None),
            P(every, None, None),
            P(every),
            P(every),
            P(every, None),
            P(every, None),
            P(),
            P(),
        ),
        out_specs=P(("y", "core"), ("x", "z")),
        check_vma=False,
    )
```

profile of v0, /device:TPU:1, one launch (start us, length us, event | category | flops | bytes accessed | tf_op | source)
XLA Modules:
  0.0 87.7 jit_solution(6755893016487939768)
XLA Ops:
  0.0 11.3 %transform.1 = f32[1280,128]{1,0:T(8,128)} custom-call(s32[1,4]{1,0:T(1,128)} %slot_v.1, s32[1,4]{1,0:T(1,128)} %slot_c.1, s32[160]{0:T(256)} %perm.1, f32[2]{0:T(128)} %energy_v.1, f32[2]{0:T(128)} %energy_c.1, bf16[2,96,9216]{2,1,0:T(8,128)(2,1)} %v_ref.1, bf16[2,96,9216]{2,1,0:T(8,128)(2,1)} %c_ref.1, bf16[48,192]{1,0:T(8,128)(2,1)} %constant.27.clone.x_table, ...), custom_call_target="tpu_custom_call" | custom-call | flops 4000000000 | bytes 9000000 | tf_op jit(solution)/shard_map/transform/pallas_call | solution.py:191
  11.3 26.2 %all_to_all.5 = f32[128,10,1,128]{3,2,1,0:T(1,128)S(1)} all-to-all(f32[128,10,1,128]{3,2,1,0:T(1,128)} %bitcast.19), channel_id=1, replica_groups=mesh['y'=4,'core'=2,'x'=4,'z'=4] {'y','core','x','z'}, dimensions={0} | all-to-all | bytes 1310720 | tf_op jit(solution)/shard_map/all_to_all | solution.py:374
  37.4 0.6 pieces.1
  38.0 1.4 %collective-permute-start.2 = (f32[160,256]{1,0:T(8,128)S(1)}, f32[160,256]{1,0:T(8,128)S(1)}, u32[]{:S(2)}, u32[]{:S(2)}) collective-permute-start(f32[160,256]{1,0:T(8,128)S(1)} %get-tuple-element.9), channel_id=1, source_target_pairs={{0,3},{1,0},{2,1},{3,2},{4,7},{5,4},{6,5},{7,6},{8,11},{9,8},{10,9... | collective-permute-start | bytes 491528 | tf_op jit(solution)/shard_map/ppermute | solution.py:368
  39.4 0.7 collective-permute-start.1
  40.1 0.5 collective-permute-start
  40.5 1.8 %collective-permute-done.2 = f32[160,256]{1,0:T(8,128)S(1)} collective-permute-done((f32[160,256]{1,0:T(8,128)S(1)}, f32[160,256]{1,0:T(8,128)S(1)}, u32[]{:S(2)}, u32[]{:S(2)}) %collective-permute-start.2) | collective-permute-done | bytes 163872 | tf_op jit(solution)/shard_map/ppermute | solution.py:368
  42.3 3.1 %collective-permute-done.1 = f32[160,256]{1,0:T(8,128)S(1)} collective-permute-done((f32[160,256]{1,0:T(8,128)S(1)}, f32[160,256]{1,0:T(8,128)S(1)}, u32[]{:S(2)}, u32[]{:S(2)}) %collective-permute-start.1) | collective-permute-done | bytes 163872 | tf_op jit(solution)/shard_map/ppermute | solution.py:368
  45.4 1.8 %collective-permute-done = f32[160,256]{1,0:T(8,128)S(1)} collective-permute-done((f32[160,256]{1,0:T(8,128)S(1)}, f32[160,256]{1,0:T(8,128)S(1)}, u32[]{:S(2)}, u32[]{:S(2)}) %collective-permute-start) | collective-permute-done | bytes 163872 | tf_op jit(solution)/shard_map/ppermute | solution.py:368
  47.2 0.6 collective-permute-start.8
  47.8 1.3 %collective-permute-start.7 = (f32[160,256]{1,0:T(8,128)S(1)}, f32[160,256]{1,0:T(8,128)S(1)}, u32[]{:S(2)}, u32[]{:S(2)}) collective-permute-start(f32[160,256]{1,0:T(8,128)S(1)} %get-tuple-element.12), channel_id=1, source_target_pairs={{0,64},{32,96},{64,0},{96,32},{1,65},{33,97},{65,1},{97,33},{2,66}... | collective-permute-start | bytes 491528 | tf_op jit(solution)/shard_map/ppermute | solution.py:344
  49.2 0.3 collective-permute-start.6
  49.5 2.0 %collective-permute-done.8 = f32[160,256]{1,0:T(8,128)S(1)} collective-permute-done((f32[160,256]{1,0:T(8,128)S(1)}, f32[160,256]{1,0:T(8,128)S(1)}, u32[]{:S(2)}, u32[]{:S(2)}) %collective-permute-start.8) | collective-permute-done | bytes 163872 | tf_op jit(solution)/shard_map/ppermute | solution.py:344
  51.4 2.1 %collective-permute-done.7 = f32[160,256]{1,0:T(8,128)S(1)} collective-permute-done((f32[160,256]{1,0:T(8,128)S(1)}, f32[160,256]{1,0:T(8,128)S(1)}, u32[]{:S(2)}, u32[]{:S(2)}) %collective-permute-start.7) | collective-permute-done | bytes 163872 | tf_op jit(solution)/shard_map/ppermute | solution.py:344
  53.6 3.8 %collective-permute-done.6 = f32[160,256]{1,0:T(8,128)S(1)} collective-permute-done((f32[160,256]{1,0:T(8,128)S(1)}, f32[160,256]{1,0:T(8,128)S(1)}, u32[]{:S(2)}, u32[]{:S(2)}) %collective-permute-start.6) | collective-permute-done | bytes 163872 | tf_op jit(solution)/shard_map/ppermute | solution.py:344
  57.4 2.2 %collective-permute-start.9 = (f32[4,160,256]{2,1,0:T(8,128)S(1)}, f32[4,160,256]{2,1,0:T(8,128)S(1)}, u32[]{:S(2)}, u32[]{:S(2)}) collective-permute-start(f32[4,160,256]{2,1,0:T(8,128)S(1)} %pad_maximum_fusion.1.mine), channel_id=1, source_target_pairs={{0,16},{16,0},{1,17},{17,1},{2,18},{18,2},{3,19},{19,3},{4,20},{20... | collective-permute-start | bytes 1966088 | tf_op jit(solution)/shard_map/ppermute | solution.py:344
  59.6 0.6 collective-permute-start.5
  60.2 2.3 %collective-permute-start.4 = (f32[4,160,256]{2,1,0:T(8,128)S(1)}, f32[4,160,256]{2,1,0:T(8,128)S(1)}, u32[]{:S(2)}, u32[]{:S(2)}) collective-permute-start(f32[4,160,256]{2,1,0:T(8,128)S(1)} %pad_maximum_fusion.refs_0_), channel_id=1, source_target_pairs={{0,12},{1,13},{2,14},{3,15},{4,0},{5,1},{6,2},{7,3},{8,4},{9,5},{1... | collective-permute-start | bytes 1966088 | tf_op jit(solution)/shard_map/ppermute | solution.py:368
  62.5 0.1 pad_add_fusion.where
  62.6 1.0 %columns.1.refs_4_ = bf16[768,1280]{1,0:T(8,128)(2,1)S(1)} custom-call(s32[4]{0:T(128)S(1)} %pad_add_fusion.where, f32[4,160,256]{2,1,0:T(8,128)S(1)} %pad_maximum_fusion.1.mine, f32[4,160,256]{2,1,0:T(8,128)S(1)} %collective-permute-done.9.theirs), custom_call_target="tpu_custom_call" | custom-call | flops 2000000 | bytes 3000000 | tf_op jit(solution)/shard_map/columns/pallas_call | solution.py:272
  63.6 7.2 %collective-permute-done.5.refs_3_ = f32[4,160,256]{2,1,0:T(8,128)S(1)} collective-permute-done((f32[4,160,256]{2,1,0:T(8,128)S(1)}, f32[4,160,256]{2,1,0:T(8,128)S(1)}, u32[]{:S(2)}, u32[]{:S(2)}) %collective-permute-start.5) | collective-permute-done | bytes 655392 | tf_op jit(solution)/shard_map/ppermute | solution.py:368
  70.9 5.2 %collective-permute-done.4.refs_2_ = f32[4,160,256]{2,1,0:T(8,128)S(1)} collective-permute-done((f32[4,160,256]{2,1,0:T(8,128)S(1)}, f32[4,160,256]{2,1,0:T(8,128)S(1)}, u32[]{:S(2)}, u32[]{:S(2)}) %collective-permute-start.4) | collective-permute-done | bytes 655392 | tf_op jit(solution)/shard_map/ppermute | solution.py:368
  76.1 1.9 %collective-permute-done.3.refs_1_ = f32[4,160,256]{2,1,0:T(8,128)} collective-permute-done((f32[4,160,256]{2,1,0:T(8,128)S(1)}, f32[4,160,256]{2,1,0:T(8,128)}, u32[]{:S(2)}, u32[]{:S(2)}) %collective-permute-start.3) | collective-permute-done | bytes 655392 | tf_op jit(solution)/shard_map/ppermute | solution.py:368
  77.9 9.7 %response.1 = f32[2560,1280]{1,0:T(8,128)} custom-call(s32[4]{0:T(128)S(1)} %pad_add_fusion.where, f32[4,160,256]{2,1,0:T(8,128)S(1)} %pad_maximum_fusion.refs_0_, f32[4,160,256]{2,1,0:T(8,128)} %collective-permute-done.3.refs_1_, f32[4,160,256]{2,1,0:T(8,128)S(1)} %collective-permute-done.4.refs_2_, f32[4,160,256]{2,1,0:T(8,128)S(1)} %collective-permute-done.5.refs_3_, ...), custom_call_target="tpu_custom_call" | custom-call | flops 5200000000 | bytes 16000000 | tf_op jit(solution)/shard_map/response/pallas_call | solution.py:320
  (6 shorter events, 0.1 us)
Async XLA Ops:
  0.0 37.4 %copy-start = (s32[128]{0:T(128)S(1)}, s32[128]{0:T(128)}, u32[]{:S(2)}) copy-start(s32[128]{0:T(128)} %param.18) | copy-start | bytes 1540
  38.0 4.2 %collective-permute-start.2 = (f32[160,256]{1,0:T(8,128)S(1)}, f32[160,256]{1,0:T(8,128)S(1)}, u32[]{:S(2)}, u32[]{:S(2)}) collective-permute-start(f32[160,256]{1,0:T(8,128)S(1)} %get-tuple-element.9), channel_id=1, source_target_pairs={{0,3},{1,0},{2,1},{3,2},{4,7},{5,4},{6,5},{7,6},{8,11},{9,8},{10,9... | collective-permute-start | bytes 491528 | tf_op jit(solution)/shard_map/ppermute | solution.py:368
  39.4 6.0 %collective-permute-start.1 = (f32[160,256]{1,0:T(8,128)S(1)}, f32[160,256]{1,0:T(8,128)S(1)}, u32[]{:S(2)}, u32[]{:S(2)}) collective-permute-start(f32[160,256]{1,0:T(8,128)S(1)} %get-tuple-element.9), channel_id=1, source_target_pairs={{0,2},{1,3},{2,0},{3,1},{4,6},{5,7},{6,4},{7,5},{8,10},{9,11},{10,... | collective-permute-start | bytes 491528 | tf_op jit(solution)/shard_map/ppermute | solution.py:368
  40.1 7.1 %collective-permute-start = (f32[160,256]{1,0:T(8,128)S(1)}, f32[160,256]{1,0:T(8,128)S(1)}, u32[]{:S(2)}, u32[]{:S(2)}) collective-permute-start(f32[160,256]{1,0:T(8,128)S(1)} %get-tuple-element.9), channel_id=1, source_target_pairs={{0,1},{1,2},{2,3},{3,0},{4,5},{5,6},{6,7},{7,4},{8,9},{9,10},{10,1... | collective-permute-start | bytes 491528 | tf_op jit(solution)/shard_map/ppermute | solution.py:368
  47.2 4.2 %collective-permute-start.8 = (f32[160,256]{1,0:T(8,128)S(1)}, f32[160,256]{1,0:T(8,128)S(1)}, u32[]{:S(2)}, u32[]{:S(2)}) collective-permute-start(f32[160,256]{1,0:T(8,128)S(1)} %get-tuple-element.12), channel_id=1, source_target_pairs={{0,96},{32,0},{64,32},{96,64},{1,97},{33,1},{65,33},{97,65},{2,98}... | collective-permute-start | bytes 491528 | tf_op jit(solution)/shard_map/ppermute | solution.py:344
  47.8 5.8 %collective-permute-start.7 = (f32[160,256]{1,0:T(8,128)S(1)}, f32[160,256]{1,0:T(8,128)S(1)}, u32[]{:S(2)}, u32[]{:S(2)}) collective-permute-start(f32[160,256]{1,0:T(8,128)S(1)} %get-tuple-element.12), channel_id=1, source_target_pairs={{0,64},{32,96},{64,0},{96,32},{1,65},{33,97},{65,1},{97,33},{2,66}... | collective-permute-start | bytes 491528 | tf_op jit(solution)/shard_map/ppermute | solution.py:344
  49.2 8.2 %collective-permute-start.6 = (f32[160,256]{1,0:T(8,128)S(1)}, f32[160,256]{1,0:T(8,128)S(1)}, u32[]{:S(2)}, u32[]{:S(2)}) collective-permute-start(f32[160,256]{1,0:T(8,128)S(1)} %get-tuple-element.12), channel_id=1, source_target_pairs={{0,32},{32,64},{64,96},{96,0},{1,33},{33,65},{65,97},{97,1},{2,34}... | collective-permute-start | bytes 491528 | tf_op jit(solution)/shard_map/ppermute | solution.py:344
  57.4 5.2 %collective-permute-start.9 = (f32[4,160,256]{2,1,0:T(8,128)S(1)}, f32[4,160,256]{2,1,0:T(8,128)S(1)}, u32[]{:S(2)}, u32[]{:S(2)}) collective-permute-start(f32[4,160,256]{2,1,0:T(8,128)S(1)} %pad_maximum_fusion.1.mine), channel_id=1, source_target_pairs={{0,16},{16,0},{1,17},{17,1},{2,18},{18,2},{3,19},{19,3},{4,20},{20... | collective-permute-start | bytes 1966088 | tf_op jit(solution)/shard_map/ppermute | solution.py:344
  59.6 11.3 %collective-permute-start.5 = (f32[4,160,256]{2,1,0:T(8,128)S(1)}, f32[4,160,256]{2,1,0:T(8,128)S(1)}, u32[]{:S(2)}, u32[]{:S(2)}) collective-permute-start(f32[4,160,256]{2,1,0:T(8,128)S(1)} %pad_maximum_fusion.refs_0_), channel_id=1, source_target_pairs={{0,8},{1,9},{2,10},{3,11},{4,12},{5,13},{6,14},{7,15},{8,0},{9,1},... | collective-permute-start | bytes 1966088 | tf_op jit(solution)/shard_map/ppermute | solution.py:368
  60.2 15.9 %collective-permute-start.4 = (f32[4,160,256]{2,1,0:T(8,128)S(1)}, f32[4,160,256]{2,1,0:T(8,128)S(1)}, u32[]{:S(2)}, u32[]{:S(2)}) collective-permute-start(f32[4,160,256]{2,1,0:T(8,128)S(1)} %pad_maximum_fusion.refs_0_), channel_id=1, source_target_pairs={{0,12},{1,13},{2,14},{3,15},{4,0},{5,1},{6,2},{7,3},{8,4},{9,5},{1... | collective-permute-start | bytes 1966088 | tf_op jit(solution)/shard_map/ppermute | solution.py:368
  62.5 15.5 %collective-permute-start.3 = (f32[4,160,256]{2,1,0:T(8,128)S(1)}, f32[4,160,256]{2,1,0:T(8,128)}, u32[]{:S(2)}, u32[]{:S(2)}) collective-permute-start(f32[4,160,256]{2,1,0:T(8,128)S(1)} %pad_maximum_fusion.refs_0_), channel_id=1, source_target_pairs={{0,4},{1,5},{2,6},{3,7},{4,8},{5,9},{6,10},{7,11},{8,12},{9,13},{1... | collective-permute-start | bytes 1966088 | tf_op jit(solution)/shard_map/ppermute | solution.py:368
where the time goes:
time: 87.9 us; the launch traced here: 87.7 us
  waiting for transfers between devices  28.8 us (33%)
  blocking collectives  26.2 us (30%)
  Pallas kernels  22.6 us (26%)
  starting transfers between devices  9.84 us (11%)
    all_to_all x1, blocking collectives, exchange(): lax.all_to_all(value, ('y', 'core', 'x', 'z'), split_axis=0, concat_axis=...  26.2 us
    ppermute x6, waiting for transfers between devices, plane_gather(): got.append(lax.ppermute(value, ('core', 'x', 'z'), pairs))  20.9 us
    pallas_call x1, Pallas kernels, transform(): pl.pallas_call(transform_kernel, name='transform', out_shape=jax.ShapeDty...  11.3 us
    pallas_call x1, Pallas kernels, response_blocks(): pl.pallas_call(functools.partial(product_kernel, count), name='response',...  9.72 us
    ppermute x4, waiting for transfers between devices, shift(): return lax.ppermute(value, axis, [(i, (i + k) % n) for i in range(n)])  7.87 us
    ppermute x6, starting transfers between devices, plane_gather(): got.append(lax.ppermute(value, ('core', 'x', 'z'), pairs))  5.38 us
    ppermute x4, starting transfers between devices, shift(): return lax.ppermute(value, axis, [(i, (i + k) % n) for i in range(n)])  4.46 us
  transfers between devices with their start and end apart: 10, of which 9 were waited for; matrix products, arithmetic and copies ran while one was open for 0% of the time, Pallas kernels for 1%

commit v1 on v0

--- a/solution.py
+++ b/solution.py
@@ -272,7 +272,7 @@
     return pl.pallas_call(
         columns_kernel,
         name="columns",
-        compiler_params=pltpu.CompilerParams(vmem_limit_bytes=16 << 20),
+        compiler_params=pltpu.CompilerParams(vmem_limit_bytes=8 << 20),
         out_shape=jax.ShapeDtypeStruct((3 * PAIRS, 1280), BF16),
         in_specs=[pl.BlockSpec(memory_space=pltpu.SMEM), vmem, vmem],
         out_specs=vmem,
@@ -320,7 +320,7 @@
     return pl.pallas_call(
         functools.partial(product_kernel, count),
         name="response",
-        compiler_params=pltpu.CompilerParams(vmem_limit_bytes=24 << 20),
+        compiler_params=pltpu.CompilerParams(vmem_limit_bytes=16 << 20),
         out_shape=jax.ShapeDtypeStruct((2560, 1280), F32),
         grid_spec=pltpu.PrefetchScalarGridSpec(
             num_scalar_prefetch=1,
@@ -384,11 +384,11 @@
     where = jnp.stack([jnp.where(core == 0, x, z), y, core, jnp.where(core == 0, z, x)])
     where = where.astype(jnp.int32)
     row = jnp.stack(plane_gather(row, 0))
-    row, column = lax.optimization_barrier((row, column))
     gathered = plane_gather(row, 1)
     mine = jnp.stack(gather(column, "y"))
     b3 = columns(where, mine, shift(mine, "core", 1))
-    return response_blocks(where, (0, 1, 3, 2), [gathered[k] for k in (0, 1, 3, 2)], b3, 1)
+    out = response_blocks(where, (0,), gathered[:1], b3, 1)
+    return response_blocks(where, (1, 3, 2), [gathered[k] for k in (1, 3, 2)], b3, 1, out)
 
 
 def solution(mesh):

time: 87.9 us -> 80.1 us (0.911)
  the two profiles are of different devices: /device:TPU:1 before, /device:TPU:8 now
where the time goes in v1:
time: 80.1 us; the launch traced here: 79.9 us
  blocking collectives  25.1 us (31%)
  Pallas kernels  24.8 us (31%)
  waiting for transfers between devices  18.5 us (23%)
  starting transfers between devices  11.3 us (14%)
    all_to_all x1, blocking collectives, exchange(): lax.all_to_all(value, ('y', 'core', 'x', 'z'), split_axis=0, concat_axis=...  25.1 us
    ppermute x6, waiting for transfers between devices, plane_gather(): got.append(lax.ppermute(value, ('core', 'x', 'z'), pairs))  15.7 us
    pallas_call x2, Pallas kernels, response_blocks(): pl.pallas_call(functools.partial(product_kernel, count), name='response',...  11.9 us
    pallas_call x1, Pallas kernels, transform(): pl.pallas_call(transform_kernel, name='transform', out_shape=jax.ShapeDty...  11.3 us
    ppermute x6, starting transfers between devices, plane_gather(): got.append(lax.ppermute(value, ('core', 'x', 'z'), pairs))  7.17 us
    ppermute x4, starting transfers between devices, shift(): return lax.ppermute(value, axis, [(i, (i + k) % n) for i in range(n)])  4.11 us
    ppermute x4, waiting for transfers between devices, shift(): return lax.ppermute(value, axis, [(i, (i + k) % n) for i in range(n)])  2.78 us
  transfers between devices with their start and end apart: 10, of which 7 were waited for; matrix products, arithmetic and copies ran while one was open for 0% of the time, Pallas kernels for 6%

profile of v1, /device:TPU:8, one launch (start us, length us, event | category | flops | bytes accessed | tf_op | source)
XLA Modules:
  0.0 79.9 jit_solution(7185593702176021181)
XLA Ops:
  0.0 11.3 %transform.1 = f32[1280,128]{1,0:T(8,128)} custom-call(s32[1,4]{1,0:T(1,128)} %slot_v.1, s32[1,4]{1,0:T(1,128)} %slot_c.1, s32[160]{0:T(256)} %perm.1, f32[2]{0:T(128)} %energy_v.1, f32[2]{0:T(128)} %energy_c.1, bf16[2,96,9216]{2,1,0:T(8,128)(2,1)} %v_ref.1, bf16[2,96,9216]{2,1,0:T(8,128)(2,1)} %c_ref.1, bf16[48,192]{1,0:T(8,128)(2,1)} %constant.27.clone.x_table, ...), custom_call_target="tpu_custom_call" | custom-call | flops 4000000000 | bytes 9000000 | tf_op jit(solution)/shard_map/transform/pallas_call | solution.py:191
  11.3 25.1 %all_to_all.5 = f32[128,10,1,128]{3,2,1,0:T(1,128)S(1)} all-to-all(f32[128,10,1,128]{3,2,1,0:T(1,128)} %bitcast.19), channel_id=1, replica_groups=mesh['y'=4,'core'=2,'x'=4,'z'=4] {'y','core','x','z'}, dimensions={0} | all-to-all | bytes 1310720 | tf_op jit(solution)/shard_map/all_to_all | solution.py:374
  36.4 0.6 pieces.1
  37.0 1.5 %collective-permute-start.8 = (f32[160,256]{1,0:T(8,128)S(1)}, f32[160,256]{1,0:T(8,128)S(1)}, u32[]{:S(2)}, u32[]{:S(2)}) collective-permute-start(f32[160,256]{1,0:T(8,128)S(1)} %get-tuple-element.8), channel_id=1, source_target_pairs={{0,96},{32,0},{64,32},{96,64},{1,97},{33,1},{65,33},{97,65},{2,98}... | collective-permute-start | bytes 491528 | tf_op jit(solution)/shard_map/ppermute | solution.py:344
  38.4 0.1 collective-permute-start.7
  38.5 2.4 %collective-permute-start.6 = (f32[160,256]{1,0:T(8,128)S(1)}, f32[160,256]{1,0:T(8,128)S(1)}, u32[]{:S(2)}, u32[]{:S(2)}) collective-permute-start(f32[160,256]{1,0:T(8,128)S(1)} %get-tuple-element.8), channel_id=1, source_target_pairs={{0,32},{32,64},{64,96},{96,0},{1,33},{33,65},{65,97},{97,1},{2,34}... | collective-permute-start | bytes 491528 | tf_op jit(solution)/shard_map/ppermute | solution.py:344
  41.0 0.4 collective-permute-start.2
  41.4 2.5 %collective-permute-start.1 = (f32[160,256]{1,0:T(8,128)S(1)}, f32[160,256]{1,0:T(8,128)S(1)}, u32[]{:S(2)}, u32[]{:S(2)}) collective-permute-start(f32[160,256]{1,0:T(8,128)S(1)} %get-tuple-element.7), channel_id=1, source_target_pairs={{0,2},{1,3},{2,0},{3,1},{4,6},{5,7},{6,4},{7,5},{8,10},{9,11},{10,... | collective-permute-start | bytes 491528 | tf_op jit(solution)/shard_map/ppermute | solution.py:368
  43.9 1.9 %collective-permute-done.8 = f32[160,256]{1,0:T(8,128)S(1)} collective-permute-done((f32[160,256]{1,0:T(8,128)S(1)}, f32[160,256]{1,0:T(8,128)S(1)}, u32[]{:S(2)}, u32[]{:S(2)}) %collective-permute-start.8) | collective-permute-done | bytes 163872 | tf_op jit(solution)/shard_map/ppermute | solution.py:344
  45.9 0.9 %collective-permute-start = (f32[160,256]{1,0:T(8,128)S(1)}, f32[160,256]{1,0:T(8,128)S(1)}, u32[]{:S(2)}, u32[]{:S(2)}) collective-permute-start(f32[160,256]{1,0:T(8,128)S(1)} %get-tuple-element.7), channel_id=1, source_target_pairs={{0,1},{1,2},{2,3},{3,0},{4,5},{5,6},{6,7},{7,4},{8,9},{9,10},{10,1... | collective-permute-start | bytes 491528 | tf_op jit(solution)/shard_map/ppermute | solution.py:368
  46.8 0.9 %collective-permute-done.6 = f32[160,256]{1,0:T(8,128)S(1)} collective-permute-done((f32[160,256]{1,0:T(8,128)S(1)}, f32[160,256]{1,0:T(8,128)S(1)}, u32[]{:S(2)}, u32[]{:S(2)}) %collective-permute-start.6) | collective-permute-done | bytes 163872 | tf_op jit(solution)/shard_map/ppermute | solution.py:344
  47.7 0.1 collective-permute-start.9
  47.8 0.0 collective-permute-done.2
  47.8 0.5 collective-permute-done.1
  48.3 4.1 %collective-permute-done = f32[160,256]{1,0:T(8,128)S(1)} collective-permute-done((f32[160,256]{1,0:T(8,128)S(1)}, f32[160,256]{1,0:T(8,128)S(1)}, u32[]{:S(2)}, u32[]{:S(2)}) %collective-permute-start) | collective-permute-done | bytes 163872 | tf_op jit(solution)/shard_map/ppermute | solution.py:368
  52.4 0.1 collective-permute-start.5
  52.5 3.2 %collective-permute-start.4 = (f32[4,160,256]{2,1,0:T(8,128)S(1)}, f32[4,160,256]{2,1,0:T(8,128)S(1)}, u32[]{:S(2)}, u32[]{:S(2)}) collective-permute-start(f32[4,160,256]{2,1,0:T(8,128)S(1)} %pad_maximum_fusion.refs_0_), channel_id=1, source_target_pairs={{0,12},{1,13},{2,14},{3,15},{4,0},{5,1},{6,2},{7,3},{8,4},{9,5},{1... | collective-permute-start | bytes 1966088 | tf_op jit(solution)/shard_map/ppermute | solution.py:368
  55.8 0.1 pad_add_fusion.where
  55.9 1.0 %columns.1.refs_1_.refs_3_ = bf16[768,1280]{1,0:T(8,128)(2,1)S(1)} custom-call(s32[4]{0:T(128)S(1)} %pad_add_fusion.where, f32[4,160,256]{2,1,0:T(8,128)S(1)} %pad_maximum_fusion.1.mine, f32[4,160,256]{2,1,0:T(8,128)S(1)} %collective-permute-done.9.theirs), custom_call_target="tpu_custom_call" | custom-call | flops 2000000 | bytes 3000000 | tf_op jit(solution)/shard_map/columns/pallas_call | solution.py:272
  56.9 3.8 %response.2.refs_4_ = f32[2560,1280]{1,0:T(8,128)} custom-call(s32[4]{0:T(128)S(1)} %pad_add_fusion.where, f32[4,160,256]{2,1,0:T(8,128)S(1)} %pad_maximum_fusion.refs_0_, bf16[768,1280]{1,0:T(8,128)(2,1)S(1)} %columns.1.refs_1_.refs_3_), custom_call_target="tpu_custom_call" | custom-call | flops 1300000000 | bytes 4000000 | tf_op jit(solution)/shard_map/response/pallas_call | solution.py:320
  60.7 4.0 %collective-permute-done.5.refs_2_ = f32[4,160,256]{2,1,0:T(8,128)S(1)} collective-permute-done((f32[4,160,256]{2,1,0:T(8,128)S(1)}, f32[4,160,256]{2,1,0:T(8,128)S(1)}, u32[]{:S(2)}, u32[]{:S(2)}) %collective-permute-start.5) | collective-permute-done | bytes 655392 | tf_op jit(solution)/shard_map/ppermute | solution.py:368
  64.7 4.0 %collective-permute-done.4.refs_1_ = f32[4,160,256]{2,1,0:T(8,128)S(1)} collective-permute-done((f32[4,160,256]{2,1,0:T(8,128)S(1)}, f32[4,160,256]{2,1,0:T(8,128)S(1)}, u32[]{:S(2)}, u32[]{:S(2)}) %collective-permute-start.4) | collective-permute-done | bytes 655392 | tf_op jit(solution)/shard_map/ppermute | solution.py:368
  68.7 3.0 %collective-permute-done.3.refs_0_ = f32[4,160,256]{2,1,0:T(8,128)} collective-permute-done((f32[4,160,256]{2,1,0:T(8,128)S(1)}, f32[4,160,256]{2,1,0:T(8,128)}, u32[]{:S(2)}, u32[]{:S(2)}) %collective-permute-start.3) | collective-permute-done | bytes 655392 | tf_op jit(solution)/shard_map/ppermute | solution.py:368
  71.7 8.1 %response.3 = f32[2560,1280]{1,0:T(8,128)} custom-call(s32[4]{0:T(128)S(1)} %pad_add_fusion.where, f32[4,160,256]{2,1,0:T(8,128)} %collective-permute-done.3.refs_0_, f32[4,160,256]{2,1,0:T(8,128)S(1)} %collective-permute-done.4.refs_1_, f32[4,160,256]{2,1,0:T(8,128)S(1)} %collective-permute-done.5.refs_2_, ...), custom_call_target="tpu_custom_call", output_to_operand_aliasing={{}: (5, {})} | custom-call | flops 3900000000 | bytes 12000000 | tf_op jit(solution)/shard_map/response/pallas_call | solution.py:320
  (7 shorter events, 0.1 us)
Async XLA Ops:
  0.0 36.4 %copy-start = (s32[128]{0:T(128)S(1)}, s32[128]{0:T(128)}, u32[]{:S(2)}) copy-start(s32[128]{0:T(128)} %param.18) | copy-start | bytes 1540
  37.0 8.9 %collective-permute-start.8 = (f32[160,256]{1,0:T(8,128)S(1)}, f32[160,256]{1,0:T(8,128)S(1)}, u32[]{:S(2)}, u32[]{:S(2)}) collective-permute-start(f32[160,256]{1,0:T(8,128)S(1)} %get-tuple-element.8), channel_id=1, source_target_pairs={{0,96},{32,0},{64,32},{96,64},{1,97},{33,1},{65,33},{97,65},{2,98}... | collective-permute-start | bytes 491528 | tf_op jit(solution)/shard_map/ppermute | solution.py:344
  38.4 8.3 %collective-permute-start.7 = (f32[160,256]{1,0:T(8,128)S(1)}, f32[160,256]{1,0:T(8,128)S(1)}, u32[]{:S(2)}, u32[]{:S(2)}) collective-permute-start(f32[160,256]{1,0:T(8,128)S(1)} %get-tuple-element.8), channel_id=1, source_target_pairs={{0,64},{32,96},{64,0},{96,32},{1,65},{33,97},{65,1},{97,33},{2,66}... | collective-permute-start | bytes 491528 | tf_op jit(solution)/shard_map/ppermute | solution.py:344
  38.5 9.1 %collective-permute-start.6 = (f32[160,256]{1,0:T(8,128)S(1)}, f32[160,256]{1,0:T(8,128)S(1)}, u32[]{:S(2)}, u32[]{:S(2)}) collective-permute-start(f32[160,256]{1,0:T(8,128)S(1)} %get-tuple-element.8), channel_id=1, source_target_pairs={{0,32},{32,64},{64,96},{96,0},{1,33},{33,65},{65,97},{97,1},{2,34}... | collective-permute-start | bytes 491528 | tf_op jit(solution)/shard_map/ppermute | solution.py:344
  41.0 6.8 %collective-permute-start.2 = (f32[160,256]{1,0:T(8,128)S(1)}, f32[160,256]{1,0:T(8,128)S(1)}, u32[]{:S(2)}, u32[]{:S(2)}) collective-permute-start(f32[160,256]{1,0:T(8,128)S(1)} %get-tuple-element.7), channel_id=1, source_target_pairs={{0,3},{1,0},{2,1},{3,2},{4,7},{5,4},{6,5},{7,6},{8,11},{9,8},{10,9... | collective-permute-start | bytes 491528 | tf_op jit(solution)/shard_map/ppermute | solution.py:368
  41.4 6.8 %collective-permute-start.1 = (f32[160,256]{1,0:T(8,128)S(1)}, f32[160,256]{1,0:T(8,128)S(1)}, u32[]{:S(2)}, u32[]{:S(2)}) collective-permute-start(f32[160,256]{1,0:T(8,128)S(1)} %get-tuple-element.7), channel_id=1, source_target_pairs={{0,2},{1,3},{2,0},{3,1},{4,6},{5,7},{6,4},{7,5},{8,10},{9,11},{10,... | collective-permute-start | bytes 491528 | tf_op jit(solution)/shard_map/ppermute | solution.py:368
  45.9 6.5 %collective-permute-start = (f32[160,256]{1,0:T(8,128)S(1)}, f32[160,256]{1,0:T(8,128)S(1)}, u32[]{:S(2)}, u32[]{:S(2)}) collective-permute-start(f32[160,256]{1,0:T(8,128)S(1)} %get-tuple-element.7), channel_id=1, source_target_pairs={{0,1},{1,2},{2,3},{3,0},{4,5},{5,6},{6,7},{7,4},{8,9},{9,10},{10,1... | collective-permute-start | bytes 491528 | tf_op jit(solution)/shard_map/ppermute | solution.py:368
  47.7 8.2 %collective-permute-start.9 = (f32[4,160,256]{2,1,0:T(8,128)S(1)}, f32[4,160,256]{2,1,0:T(8,128)S(1)}, u32[]{:S(2)}, u32[]{:S(2)}) collective-permute-start(f32[4,160,256]{2,1,0:T(8,128)S(1)} %pad_maximum_fusion.1.mine), channel_id=1, source_target_pairs={{0,16},{16,0},{1,17},{17,1},{2,18},{18,2},{3,19},{19,3},{4,20},{20... | collective-permute-start | bytes 1966088 | tf_op jit(solution)/shard_map/ppermute | solution.py:344
  52.4 12.3 %collective-permute-start.5 = (f32[4,160,256]{2,1,0:T(8,128)S(1)}, f32[4,160,256]{2,1,0:T(8,128)S(1)}, u32[]{:S(2)}, u32[]{:S(2)}) collective-permute-start(f32[4,160,256]{2,1,0:T(8,128)S(1)} %pad_maximum_fusion.refs_0_), channel_id=1, source_target_pairs={{0,8},{1,9},{2,10},{3,11},{4,12},{5,13},{6,14},{7,15},{8,0},{9,1},... | collective-permute-start | bytes 1966088 | tf_op jit(solution)/shard_map/ppermute | solution.py:368
  52.5 16.2 %collective-permute-start.4 = (f32[4,160,256]{2,1,0:T(8,128)S(1)}, f32[4,160,256]{2,1,0:T(8,128)S(1)}, u32[]{:S(2)}, u32[]{:S(2)}) collective-permute-start(f32[4,160,256]{2,1,0:T(8,128)S(1)} %pad_maximum_fusion.refs_0_), channel_id=1, source_target_pairs={{0,12},{1,13},{2,14},{3,15},{4,0},{5,1},{6,2},{7,3},{8,4},{9,5},{1... | collective-permute-start | bytes 1966088 | tf_op jit(solution)/shard_map/ppermute | solution.py:368
  55.8 16.0 %collective-permute-start.3 = (f32[4,160,256]{2,1,0:T(8,128)S(1)}, f32[4,160,256]{2,1,0:T(8,128)}, u32[]{:S(2)}, u32[]{:S(2)}) collective-permute-start(f32[4,160,256]{2,1,0:T(8,128)S(1)} %pad_maximum_fusion.refs_0_), channel_id=1, source_target_pairs={{0,4},{1,5},{2,6},{3,7},{4,8},{5,9},{6,10},{7,11},{8,12},{9,13},{1... | collective-permute-start | bytes 1966088 | tf_op jit(solution)/shard_map/ppermute | solution.py:368

commit v2 on v1

--- a/solution.py
+++ b/solution.py
@@ -129,14 +129,12 @@
     zl,
     natural,
     ordered,
-    v_wide,
-    c_wide,
 ):
     step = pl.program_id(0)
-    v_wide[...] = v_ref[...].astype(F32)
-    c_wide[...] = c_ref[...].astype(F32)
     for k in range(CAP):
-        high, low = split(v_wide[slot_v[0, k]] * c_wide[slot_c[0, k]])
+        left = v_ref[slot_v[0, k]].astype(F32)
+        right = c_ref[slot_c[0, k]].astype(F32)
+        high, low = split(left * right)
         x_part = dot(x_table[...], jnp.concatenate([high, low], 0))
         x_part = x_part[:GROWS] + x_part[GROWS:]
         for g in range(3):
@@ -202,8 +200,6 @@
                 pltpu.VMEM((3, NB * 8, CAP * Q), BF16),
                 pltpu.VMEM((8 * NSTICK, LANES), F32),
                 pltpu.VMEM((8 * NSTICK, LANES), F32),
-                pltpu.VMEM((2, NG, CHUNK), F32),
-                pltpu.VMEM((2, NG, CHUNK), F32),
             ],
         ),
         cost_estimate=pl.CostEstimate(

time: 80.1 us -> 80 us (level)
  no operation moved by 1% of the time
where the time goes in v2:
time: 80 us; the launch traced here: 79.8 us
  blocking collectives  25.1 us (31%)
  Pallas kernels  24.7 us (31%)
  waiting for transfers between devices  18.5 us (23%)
  starting transfers between devices  11.3 us (14%)
    all_to_all x1, blocking collectives, exchange(): lax.all_to_all(value, ('y', 'core', 'x', 'z'), split_axis=0, concat_axis=...  25.1 us
    ppermute x6, waiting for transfers between devices, plane_gather(): got.append(lax.ppermute(value, ('core', 'x', 'z'), pairs))  15.7 us
    pallas_call x2, Pallas kernels, response_blocks(): pl.pallas_call(functools.partial(product_kernel, count), name='response',...  11.9 us
    pallas_call x1, Pallas kernels, transform(): pl.pallas_call(transform_kernel, name='transform', out_shape=jax.ShapeDty...  11.2 us
    ppermute x6, starting transfers between devices, plane_gather(): got.append(lax.ppermute(value, ('core', 'x', 'z'), pairs))  7.17 us
    ppermute x4, starting transfers between devices, shift(): return lax.ppermute(value, axis, [(i, (i + k) % n) for i in range(n)])  4.11 us
    ppermute x4, waiting for transfers between devices, shift(): return lax.ppermute(value, axis, [(i, (i + k) % n) for i in range(n)])  2.78 us
  transfers between devices with their start and end apart: 10, of which 7 were waited for; matrix products, arithmetic and copies ran while one was open for 0% of the time, Pallas kernels for 6%

profile of v2, /device:TPU:8, one launch (start us, length us, event | category | flops | bytes accessed | tf_op | source)
XLA Modules:
  0.0 79.8 jit_solution(14848844416883677717)
XLA Ops:
  0.0 11.2 %transform.1 = f32[1280,128]{1,0:T(8,128)} custom-call(s32[1,4]{1,0:T(1,128)} %slot_v.1, s32[1,4]{1,0:T(1,128)} %slot_c.1, s32[160]{0:T(256)} %perm.1, f32[2]{0:T(128)} %energy_v.1, f32[2]{0:T(128)} %energy_c.1, bf16[2,96,9216]{2,1,0:T(8,128)(2,1)} %v_ref.1, bf16[2,96,9216]{2,1,0:T(8,128)(2,1)} %c_ref.1, bf16[48,192]{1,0:T(8,128)(2,1)} %constant.27.clone.x_table, ...), custom_call_target="tpu_custom_call" | custom-call | flops 4000000000 | bytes 9000000 | tf_op jit(solution)/shard_map/transform/pallas_call | solution.py:189
  11.2 25.1 %all_to_all.5 = f32[128,10,1,128]{3,2,1,0:T(1,128)S(1)} all-to-all(f32[128,10,1,128]{3,2,1,0:T(1,128)} %bitcast.19), channel_id=1, replica_groups=mesh['y'=4,'core'=2,'x'=4,'z'=4] {'y','core','x','z'}, dimensions={0} | all-to-all | bytes 1310720 | tf_op jit(solution)/shard_map/all_to_all | solution.py:370
  36.2 0.6 pieces.1
  36.8 1.5 %collective-permute-start.8 = (f32[160,256]{1,0:T(8,128)S(1)}, f32[160,256]{1,0:T(8,128)S(1)}, u32[]{:S(2)}, u32[]{:S(2)}) collective-permute-start(f32[160,256]{1,0:T(8,128)S(1)} %get-tuple-element.8), channel_id=1, source_target_pairs={{0,96},{32,0},{64,32},{96,64},{1,97},{33,1},{65,33},{97,65},{2,98}... | collective-permute-start | bytes 491528 | tf_op jit(solution)/shard_map/ppermute | solution.py:340
  38.3 0.1 collective-permute-start.7
  38.4 2.4 %collective-permute-start.6 = (f32[160,256]{1,0:T(8,128)S(1)}, f32[160,256]{1,0:T(8,128)S(1)}, u32[]{:S(2)}, u32[]{:S(2)}) collective-permute-start(f32[160,256]{1,0:T(8,128)S(1)} %get-tuple-element.8), channel_id=1, source_target_pairs={{0,32},{32,64},{64,96},{96,0},{1,33},{33,65},{65,97},{97,1},{2,34}... | collective-permute-start | bytes 491528 | tf_op jit(solution)/shard_map/ppermute | solution.py:340
  40.9 0.4 collective-permute-start.2
  41.3 2.5 %collective-permute-start.1 = (f32[160,256]{1,0:T(8,128)S(1)}, f32[160,256]{1,0:T(8,128)S(1)}, u32[]{:S(2)}, u32[]{:S(2)}) collective-permute-start(f32[160,256]{1,0:T(8,128)S(1)} %get-tuple-element.7), channel_id=1, source_target_pairs={{0,2},{1,3},{2,0},{3,1},{4,6},{5,7},{6,4},{7,5},{8,10},{9,11},{10,... | collective-permute-start | bytes 491528 | tf_op jit(solution)/shard_map/ppermute | solution.py:364
  43.8 1.9 %collective-permute-done.8 = f32[160,256]{1,0:T(8,128)S(1)} collective-permute-done((f32[160,256]{1,0:T(8,128)S(1)}, f32[160,256]{1,0:T(8,128)S(1)}, u32[]{:S(2)}, u32[]{:S(2)}) %collective-permute-start.8) | collective-permute-done | bytes 163872 | tf_op jit(solution)/shard_map/ppermute | solution.py:340
  45.7 0.9 %collective-permute-start = (f32[160,256]{1,0:T(8,128)S(1)}, f32[160,256]{1,0:T(8,128)S(1)}, u32[]{:S(2)}, u32[]{:S(2)}) collective-permute-start(f32[160,256]{1,0:T(8,128)S(1)} %get-tuple-element.7), channel_id=1, source_target_pairs={{0,1},{1,2},{2,3},{3,0},{4,5},{5,6},{6,7},{7,4},{8,9},{9,10},{10,1... | collective-permute-start | bytes 491528 | tf_op jit(solution)/shard_map/ppermute | solution.py:364
  46.6 0.0 collective-permute-done.7
  46.6 0.9 %collective-permute-done.6 = f32[160,256]{1,0:T(8,128)S(1)} collective-permute-done((f32[160,256]{1,0:T(8,128)S(1)}, f32[160,256]{1,0:T(8,128)S(1)}, u32[]{:S(2)}, u32[]{:S(2)}) %collective-permute-start.6) | collective-permute-done | bytes 163872 | tf_op jit(solution)/shard_map/ppermute | solution.py:340
  47.6 0.1 collective-permute-start.9
  47.7 0.5 collective-permute-done.1
  48.1 4.1 %collective-permute-done = f32[160,256]{1,0:T(8,128)S(1)} collective-permute-done((f32[160,256]{1,0:T(8,128)S(1)}, f32[160,256]{1,0:T(8,128)S(1)}, u32[]{:S(2)}, u32[]{:S(2)}) %collective-permute-start) | collective-permute-done | bytes 163872 | tf_op jit(solution)/shard_map/ppermute | solution.py:364
  52.3 0.1 collective-permute-start.5
  52.4 3.2 %collective-permute-start.4 = (f32[4,160,256]{2,1,0:T(8,128)S(1)}, f32[4,160,256]{2,1,0:T(8,128)S(1)}, u32[]{:S(2)}, u32[]{:S(2)}) collective-permute-start(f32[4,160,256]{2,1,0:T(8,128)S(1)} %pad_maximum_fusion.refs_0_), channel_id=1, source_target_pairs={{0,12},{1,13},{2,14},{3,15},{4,0},{5,1},{6,2},{7,3},{8,4},{9,5},{1... | collective-permute-start | bytes 1966088 | tf_op jit(solution)/shard_map/ppermute | solution.py:364
  55.7 0.1 pad_add_fusion.where
  55.7 1.0 %columns.1.refs_1_.refs_3_ = bf16[768,1280]{1,0:T(8,128)(2,1)S(1)} custom-call(s32[4]{0:T(128)S(1)} %pad_add_fusion.where, f32[4,160,256]{2,1,0:T(8,128)S(1)} %pad_maximum_fusion.1.mine, f32[4,160,256]{2,1,0:T(8,128)S(1)} %collective-permute-done.9.theirs), custom_call_target="tpu_custom_call" | custom-call | flops 2000000 | bytes 3000000 | tf_op jit(solution)/shard_map/columns/pallas_call | solution.py:268
  56.8 3.8 %response.2.refs_4_ = f32[2560,1280]{1,0:T(8,128)} custom-call(s32[4]{0:T(128)S(1)} %pad_add_fusion.where, f32[4,160,256]{2,1,0:T(8,128)S(1)} %pad_maximum_fusion.refs_0_, bf16[768,1280]{1,0:T(8,128)(2,1)S(1)} %columns.1.refs_1_.refs_3_), custom_call_target="tpu_custom_call" | custom-call | flops 1300000000 | bytes 4000000 | tf_op jit(solution)/shard_map/response/pallas_call | solution.py:316
  60.6 4.0 %collective-permute-done.5.refs_2_ = f32[4,160,256]{2,1,0:T(8,128)S(1)} collective-permute-done((f32[4,160,256]{2,1,0:T(8,128)S(1)}, f32[4,160,256]{2,1,0:T(8,128)S(1)}, u32[]{:S(2)}, u32[]{:S(2)}) %collective-permute-start.5) | collective-permute-done | bytes 655392 | tf_op jit(solution)/shard_map/ppermute | solution.py:364
  64.6 4.0 %collective-permute-done.4.refs_1_ = f32[4,160,256]{2,1,0:T(8,128)S(1)} collective-permute-done((f32[4,160,256]{2,1,0:T(8,128)S(1)}, f32[4,160,256]{2,1,0:T(8,128)S(1)}, u32[]{:S(2)}, u32[]{:S(2)}) %collective-permute-start.4) | collective-permute-done | bytes 655392 | tf_op jit(solution)/shard_map/ppermute | solution.py:364
  68.6 3.0 %collective-permute-done.3.refs_0_ = f32[4,160,256]{2,1,0:T(8,128)} collective-permute-done((f32[4,160,256]{2,1,0:T(8,128)S(1)}, f32[4,160,256]{2,1,0:T(8,128)}, u32[]{:S(2)}, u32[]{:S(2)}) %collective-permute-start.3) | collective-permute-done | bytes 655392 | tf_op jit(solution)/shard_map/ppermute | solution.py:364
  71.6 8.1 %response.3 = f32[2560,1280]{1,0:T(8,128)} custom-call(s32[4]{0:T(128)S(1)} %pad_add_fusion.where, f32[4,160,256]{2,1,0:T(8,128)} %collective-permute-done.3.refs_0_, f32[4,160,256]{2,1,0:T(8,128)S(1)} %collective-permute-done.4.refs_1_, f32[4,160,256]{2,1,0:T(8,128)S(1)} %collective-permute-done.5.refs_2_, ...), custom_call_target="tpu_custom_call", output_to_operand_aliasing={{}: (5, {})} | custom-call | flops 3900000000 | bytes 12000000 | tf_op jit(solution)/shard_map/response/pallas_call | solution.py:316
  (7 shorter events, 0.1 us)
Async XLA Ops:
  0.0 36.2 %copy-start = (s32[128]{0:T(128)S(1)}, s32[128]{0:T(128)}, u32[]{:S(2)}) copy-start(s32[128]{0:T(128)} %param.18) | copy-start | bytes 1540
  36.8 8.9 %collective-permute-start.8 = (f32[160,256]{1,0:T(8,128)S(1)}, f32[160,256]{1,0:T(8,128)S(1)}, u32[]{:S(2)}, u32[]{:S(2)}) collective-permute-start(f32[160,256]{1,0:T(8,128)S(1)} %get-tuple-element.8), channel_id=1, source_target_pairs={{0,96},{32,0},{64,32},{96,64},{1,97},{33,1},{65,33},{97,65},{2,98}... | collective-permute-start | bytes 491528 | tf_op jit(solution)/shard_map/ppermute | solution.py:340
  38.3 8.3 %collective-permute-start.7 = (f32[160,256]{1,0:T(8,128)S(1)}, f32[160,256]{1,0:T(8,128)S(1)}, u32[]{:S(2)}, u32[]{:S(2)}) collective-permute-start(f32[160,256]{1,0:T(8,128)S(1)} %get-tuple-element.8), channel_id=1, source_target_pairs={{0,64},{32,96},{64,0},{96,32},{1,65},{33,97},{65,1},{97,33},{2,66}... | collective-permute-start | bytes 491528 | tf_op jit(solution)/shard_map/ppermute | solution.py:340
  38.4 9.1 %collective-permute-start.6 = (f32[160,256]{1,0:T(8,128)S(1)}, f32[160,256]{1,0:T(8,128)S(1)}, u32[]{:S(2)}, u32[]{:S(2)}) collective-permute-start(f32[160,256]{1,0:T(8,128)S(1)} %get-tuple-element.8), channel_id=1, source_target_pairs={{0,32},{32,64},{64,96},{96,0},{1,33},{33,65},{65,97},{97,1},{2,34}... | collective-permute-start | bytes 491528 | tf_op jit(solution)/shard_map/ppermute | solution.py:340
  40.9 6.8 %collective-permute-start.2 = (f32[160,256]{1,0:T(8,128)S(1)}, f32[160,256]{1,0:T(8,128)S(1)}, u32[]{:S(2)}, u32[]{:S(2)}) collective-permute-start(f32[160,256]{1,0:T(8,128)S(1)} %get-tuple-element.7), channel_id=1, source_target_pairs={{0,3},{1,0},{2,1},{3,2},{4,7},{5,4},{6,5},{7,6},{8,11},{9,8},{10,9... | collective-permute-start | bytes 491528 | tf_op jit(solution)/shard_map/ppermute | solution.py:364
  41.3 6.8 %collective-permute-start.1 = (f32[160,256]{1,0:T(8,128)S(1)}, f32[160,256]{1,0:T(8,128)S(1)}, u32[]{:S(2)}, u32[]{:S(2)}) collective-permute-start(f32[160,256]{1,0:T(8,128)S(1)} %get-tuple-element.7), channel_id=1, source_target_pairs={{0,2},{1,3},{2,0},{3,1},{4,6},{5,7},{6,4},{7,5},{8,10},{9,11},{10,... | collective-permute-start | bytes 491528 | tf_op jit(solution)/shard_map/ppermute | solution.py:364
  45.7 6.5 %collective-permute-start = (f32[160,256]{1,0:T(8,128)S(1)}, f32[160,256]{1,0:T(8,128)S(1)}, u32[]{:S(2)}, u32[]{:S(2)}) collective-permute-start(f32[160,256]{1,0:T(8,128)S(1)} %get-tuple-element.7), channel_id=1, source_target_pairs={{0,1},{1,2},{2,3},{3,0},{4,5},{5,6},{6,7},{7,4},{8,9},{9,10},{10,1... | collective-permute-start | bytes 491528 | tf_op jit(solution)/shard_map/ppermute | solution.py:364
  47.6 8.2 %collective-permute-start.9 = (f32[4,160,256]{2,1,0:T(8,128)S(1)}, f32[4,160,256]{2,1,0:T(8,128)S(1)}, u32[]{:S(2)}, u32[]{:S(2)}) collective-permute-start(f32[4,160,256]{2,1,0:T(8,128)S(1)} %pad_maximum_fusion.1.mine), channel_id=1, source_target_pairs={{0,16},{16,0},{1,17},{17,1},{2,18},{18,2},{3,19},{19,3},{4,20},{20... | collective-permute-start | bytes 1966088 | tf_op jit(solution)/shard_map/ppermute | solution.py:340
  52.3 12.3 %collective-permute-start.5 = (f32[4,160,256]{2,1,0:T(8,128)S(1)}, f32[4,160,256]{2,1,0:T(8,128)S(1)}, u32[]{:S(2)}, u32[]{:S(2)}) collective-permute-start(f32[4,160,256]{2,1,0:T(8,128)S(1)} %pad_maximum_fusion.refs_0_), channel_id=1, source_target_pairs={{0,8},{1,9},{2,10},{3,11},{4,12},{5,13},{6,14},{7,15},{8,0},{9,1},... | collective-permute-start | bytes 1966088 | tf_op jit(solution)/shard_map/ppermute | solution.py:364
  52.4 16.2 %collective-permute-start.4 = (f32[4,160,256]{2,1,0:T(8,128)S(1)}, f32[4,160,256]{2,1,0:T(8,128)S(1)}, u32[]{:S(2)}, u32[]{:S(2)}) collective-permute-start(f32[4,160,256]{2,1,0:T(8,128)S(1)} %pad_maximum_fusion.refs_0_), channel_id=1, source_target_pairs={{0,12},{1,13},{2,14},{3,15},{4,0},{5,1},{6,2},{7,3},{8,4},{9,5},{1... | collective-permute-start | bytes 1966088 | tf_op jit(solution)/shard_map/ppermute | solution.py:364
  55.7 16.0 %collective-permute-start.3 = (f32[4,160,256]{2,1,0:T(8,128)S(1)}, f32[4,160,256]{2,1,0:T(8,128)}, u32[]{:S(2)}, u32[]{:S(2)}) collective-permute-start(f32[4,160,256]{2,1,0:T(8,128)S(1)} %pad_maximum_fusion.refs_0_), channel_id=1, source_target_pairs={{0,4},{1,5},{2,6},{3,7},{4,8},{5,9},{6,10},{7,11},{8,12},{9,13},{1... | collective-permute-start | bytes 1966088 | tf_op jit(solution)/shard_map/ppermute | solution.py:364
